TPU v7x, 32 devices: a whole 2x2x4 slice. The times are simulated.
32 devices in a mesh: grp: 2 (over x), row: 4 (over y, core), diag: 4 (over z).
Axes of the slice: x: 2, y: 2, z: 4, core: 2. Of those that a mesh axis runs over, the one named last changes fastest.
Arguments:
- emb_rows: bfloat16 [32, 1024], P(None, ('grp', 'row')), parts along dimension 1, may hold values from -6 to 6
- emb_cols: bfloat16 [32, 1024], P(None, ('grp', 'row')), parts along dimension 1, may hold values from -6 to 6
- kernel: bfloat16 [3, 3, 32, 32], replicated, may hold values from -0.375 to 0.375
- bias: float32 [32], replicated, may hold values from -3 to 3
- cotangent: bfloat16 [32, 1024, 512], P(None, ('grp', 'row'), 'diag'), parts along dimension 1, may hold values from -6 to 6
- valid: int32 [1024], P(('grp', 'row')), parts along dimension 0, may hold values 0 or 1
- dilation: int32 [2], P('grp'), parts along dimension 0, may hold values from 1 to 4
- band: int32 [2], P('grp'), parts along dimension 0, may hold values from 384 to 512
Outputs:
- pair_out: bfloat16 [32, 1024, 512], P(None, ('grp', 'row'), 'diag'), parts along dimension 1
- row_grad: float32 [32, 1024], P(None, ('grp', 'row')), parts along dimension 1
- col_grad: float32 [32, 1024], P(None, ('grp', 'row')), parts along dimension 1
- kernel_grad: float32 [6, 3, 32, 32], P('grp'), parts along dimension 0
- bias_grad: float32 [64], P('grp'), parts along dimension 0
There are 2 independent parts, one for each index of `grp`. A program takes and returns all parts, laid end to end along the dimension named above; an argument that names none is the same for every part. Nothing has to cross between parts.
All inputs are finite; a program needn't handle non-finite values. No bound on the sum of `valid` on one device may be relied on, other than what follows from the above.
Results may differ from a plain program's by a relative error of at most 0.0032.
Values may be sent and summed in bfloat16 or wider, within the bound.
A program may use at most 128 MiB of HBM per device.

v0:
```python
import functools

import jax
import jax.numpy as jnp
from jax import lax
from jax.experimental import pallas as pl
from jax.experimental.pallas import tpu as pltpu
from jax.sharding import PartitionSpec as P

MAXDIL = 4
RG = 8
S2PI = 0.7978845608028654
CUBIC = 0.044715


def with_halo(array, axis, dim, width):
    size, length = (lax.axis_size(axis), array.shape[dim])
    up = [(i, i + 1) for i in range(size - 1)]
    down = [(j, i) for i, j in up]
    last = lax.slice_in_dim(array, length - width, length, axis=dim)
    initial = lax.slice_in_dim(array, 0, width, axis=dim)
    return lax.ppermute(last, axis, up), lax.ppermute(initial, axis, down)


def pair_kernel(
    par, vr, rows, cols, vcol, cot, halo, kf, kb, bias,
    out, rsum, csum, kgrad,
    act3, gz3, gzm, hid, der, tf, tb, kacc, bacc,
):
    n = out.shape[0]
    ch = out.shape[1]
    wide = 2 * n
    r, w, d0 = par[0], par[1], par[2]
    groups = n // RG
    blk = RG * ch
    lane1 = lax.broadcasted_iota(jnp.int32, (RG, wide), 1)

    def offsets(i):
        d = lane1 - i
        d = jnp.where(d < -(n // 2), d + wide, d)
        return jnp.where(d >= wide - n // 2, d - wide, d)

    def validity(e, i, side):
        d = offsets(i)
        inside = (d + d0 >= 0) & (d + d0 < w)
        v = jnp.where(inside, vcol[side] * vr[e], 0.0)
        return v, d

    kblk = lax.broadcasted_iota(jnp.int32, (ch, 2 * blk), 1) // ch
    for b in range(3):
        for ii in range(RG):
            f = jnp.zeros((ch, 2 * blk), jnp.float32)
            g = jnp.zeros((ch, 2 * blk), jnp.float32)
            for a in range(3):
                f = jnp.where(kblk == ii + MAXDIL + (a - 1) * r, kf[3 * a + b].astype(jnp.float32), f)
                g = jnp.where(kblk == ii + MAXDIL - (a - 1) * r, kb[3 * a + b].astype(jnp.float32), g)
            tf[b, ii * ch : (ii + 1) * ch, :] = f.astype(jnp.bfloat16)
            tb[b, ii * ch : (ii + 1) * ch, :] = g.astype(jnp.bfloat16)

    def phase_a(gi, carry):
        side = jnp.where(gi * RG > n // 2, 1, 0)
        for ii in range(RG):
            e = gi * RG + ii
            i = e - MAXDIL
            v8, d8 = validity(e, i, side)
            v = jnp.concatenate([v8] * (ch // RG), axis=0)
            d = jnp.concatenate([d8] * (ch // RG), axis=0)
            rw = rows[e].astype(jnp.float32)
            h = (jnp.concatenate([rw, rw], axis=1) + cols[side]) * v
            h2 = h * h
            t = jnp.tanh(S2PI * h * (1.0 + CUBIC * h2))
            cdf = 0.5 * (1.0 + t)
            act = h * cdf
            dg = cdf + (0.5 * S2PI) * h * (1.0 - t * t) * (1.0 + 3.0 * CUBIC * h2)
            at = pl.ds(pl.multiple_of(e * ch, ch), ch)
            act3[1, at, :] = act.astype(jnp.bfloat16)
            act3[0, at, :] = pltpu.roll(act, r, 1).astype(jnp.bfloat16)
            act3[2, at, :] = pltpu.roll(act, wide - r, 1).astype(jnp.bfloat16)
            ct = jnp.concatenate([cot[e].astype(jnp.float32), halo[e].astype(jnp.float32)], axis=1)
            gz = pltpu.roll(ct, lax.rem(i + wide, wide), 1) * v
            main = (d >= 0) & (d < n)
            gz3[1, at, :] = gz.astype(jnp.bfloat16)
            gz3[2, at, :] = pltpu.roll(gz, r, 1).astype(jnp.bfloat16)
            gz3[0, at, :] = pltpu.roll(gz, wide - r, 1).astype(jnp.bfloat16)
            gzm[at, :] = jnp.where(main, gz, 0.0).astype(jnp.bfloat16)
            hid[at, :] = h
            der[at, :] = jnp.where(main, dg * v, 0.0)
        return carry

    lax.fori_loop(0, groups + 1, phase_a, 0)

    kacc[...] = jnp.zeros_like(kacc)
    bacc[...] = jnp.zeros_like(bacc)
    rsum[...] = jnp.zeros_like(rsum)
    csum[...] = jnp.zeros_like(csum)
    lane_n = lax.broadcasted_iota(jnp.int32, (ch, n), 1)

    def phase_b(gi, carry):
        big = pl.ds(pl.multiple_of(gi * blk, blk), 2 * blk)
        own = pl.ds(pl.multiple_of(gi * blk + MAXDIL * ch, MAXDIL * ch), blk)
        z = jnp.zeros((blk, wide), jnp.float32)
        da = jnp.zeros((blk, wide), jnp.float32)
        g = gzm[own, :]
        for b in range(3):
            x = act3[b, big, :]
            z = z + jnp.dot(tf[b], x, preferred_element_type=jnp.float32)
            da = da + jnp.dot(tb[b], gz3[b, big, :], preferred_element_type=jnp.float32)
            kacc[b] += lax.dot_general(g, x, (((1,), (1,)), ((), ())), preferred_element_type=jnp.float32)
        gf = g.astype(jnp.float32)
        dx = gf + der[own, :] * da
        hz = hid[own, :] + z
        bsum, cs, rs = bacc[...], csum[...], rsum[...]
        for ii in range(RG):
            i = gi * RG + ii
            side = jnp.where(i + MAXDIL >= (n // 2 // RG) * RG + RG, 1, 0)
            v8, _ = validity(i + MAXDIL, i, side)
            v = jnp.concatenate([v8] * (ch // RG), axis=0)
            sl = slice(ii * ch, (ii + 1) * ch)
            po = (hz[sl] + bias[...]) * v
            out[i] = pltpu.roll(po, lax.rem(wide - i, wide), 1)[:, :n].astype(jnp.bfloat16)
            bsum = bsum + gf[sl]
            cs = cs + dx[sl]
            tot = jnp.sum(dx[sl], axis=1, keepdims=True)
            rs = jnp.where(lane_n == i, tot, rs)
        bacc[...] = bsum
        csum[...] = cs
        rsum[...] = rs
        return carry

    lax.fori_loop(0, groups, phase_b, 0)

    lanes = lax.broadcasted_iota(jnp.int32, (RG, 128), 1) // ch
    pieces = []
    for a in range(3):
        for b in range(3):
            s = jnp.zeros((ch, 2 * blk), jnp.float32)
            for ii in range(RG):
                s = s + jnp.where(kblk == ii + MAXDIL + (a - 1) * r, kacc[b, ii * ch : (ii + 1) * ch, :], 0.0)
            f = s[:, :128]
            for m in range(1, 2 * blk // 128):
                f = f + s[:, m * 128 : (m + 1) * 128]
            f = f + pltpu.roll(f, 64, 1)
            f = f + pltpu.roll(f, 32, 1)
            pieces += [f[m * RG : (m + 1) * RG] for m in range(ch // RG)]
    bt = jnp.broadcast_to(jnp.sum(bacc[...], axis=1, keepdims=True), (ch, 128))
    count = len(pieces) // 4
    for s in range(count):
        piece = pieces[s]
        for m in range(1, 4):
            piece = jnp.where(lanes == m, pieces[m * count + s], piece)
        kgrad[s] = piece
    piece = bt[:RG]
    for m in range(1, 4):
        piece = jnp.where(lanes == m, bt[m * RG : (m + 1) * RG], piece)
    kgrad[count] = piece


def sum_kernel(
    R, T, kg, row, col, kg_out, rc_out,
    kbuf, rbuf, abuf, bbuf, ksum, rcsum, kres, rcres,
    ks, kr, rs, rr, as_, ar, bs, br, k2s, k2r, r2s, r2r,
):
    N = R * T
    K, Z = kg.shape[0], row.shape[0]
    q, t = lax.axis_index("row"), lax.axis_index("diag")
    me = q * T + t

    def loop(count, body):
        def step(p, c):
            body(p)
            return c
        lax.fori_loop(0, count, step, 0)

    def send(src, dst, ss, sr, dq, dt):
        return pltpu.make_async_remote_copy(
            src_ref=src, dst_ref=dst, send_sem=ss, recv_sem=sr,
            device_id={"row": dq, "diag": dt}, device_id_type=pl.DeviceIdType.MESH,
        )

    barrier = pltpu.get_barrier_semaphore()

    def greet(p):
        @pl.when(p != me)
        def _():
            pl.semaphore_signal(barrier, inc=1, device_id={"row": p // T, "diag": p % T},
                                device_id_type=pl.DeviceIdType.MESH)
    loop(N, greet)
    pl.semaphore_wait(barrier, N - 1)

    def k1(k):
        return send(kg.at[k], kbuf.at[me], ks.at[k], kr.at[me], k // T, k % T)

    def r1(z):
        return send(row.at[z], rbuf.at[t], rs.at[z], rr.at[t], q, z)

    def a1(z):
        return send(col.at[0, z], abuf.at[q], as_.at[z], ar.at[q], q + t, z)

    def b1(z):
        return send(col.at[1, z], bbuf.at[q], bs.at[z], br.at[q], q + t + 1, z)

    def first(act):
        for k in range(K):
            @pl.when(me != k)
            def _():
                act(k1(k))
        for z in range(Z):
            @pl.when(t != z)
            def _():
                act(r1(z))

            @pl.when((q + t < R) & ((t != 0) | (z != 0)))
            def _():
                act(a1(z))

            @pl.when(q + t + 1 < R)
            def _():
                act(b1(z))

    first(lambda c: c.start())

    def got(buf, sem):
        send(buf, buf, sem, sem, q, t).wait_recv()

    def k2(p):
        return send(ksum, kres.at[me], k2s.at[p], k2r.at[me], p // T, p % T)

    def r2(p):
        return send(rcsum, rcres.at[t], r2s.at[p], r2r.at[t], q, p)

    def second(act):
        @pl.when(me < K)
        def _():
            def one(p):
                @pl.when(p != me)
                def _():
                    act(k2(p))
            loop(N, one)

        @pl.when(t < Z)
        def _():
            def one(p):
                @pl.when(p != t)
                def _():
                    act(r2(p))
            loop(T, one)

    @pl.when(me < K)
    def _():
        ksum[...] = kg[me]

        def take(p):
            @pl.when(p != me)
            def _():
                got(kbuf.at[p], kr.at[p])
                ksum[...] += kbuf[p]
        loop(N, take)
        kres[me] = ksum[...]

    @pl.when(t < Z)
    def _():
        rcsum[0] = row[t]
        rcsum[1] = jnp.zeros_like(rcsum[1])

        def take(p):
            @pl.when(p != t)
            def _():
                got(rbuf.at[p], rr.at[p])
                rcsum[0] += rbuf[p]
        loop(T, take)

        @pl.when(t == 0)
        def _():
            rcsum[1] = col[0, 0]

        def take_col(p):
            @pl.when((p <= q) & (q - p < T) & ((p != q) | (t != 0)))
            def _():
                got(abuf.at[p], ar.at[p])
                rcsum[1] += abuf[p]

            @pl.when((p <= q - 1) & (q - 1 - p < T))
            def _():
                got(bbuf.at[p], br.at[p])
                rcsum[1] += bbuf[p]
        loop(R, take_col)
        rcres[t] = rcsum[...]

    second(lambda c: c.start())
    for k in range(K):
        @pl.when(me != k)
        def _():
            got(kres.at[k], k2r.at[k])
    for z in range(Z):
        @pl.when(t != z)
        def _():
            got(rcres.at[z], r2r.at[z])
    kg_out[...] = kres[...]
    rc_out[...] = rcres[...]
    first(lambda c: c.wait_send())
    second(lambda c: c.wait_send())


def local(emb_rows, emb_cols, kernel, bias, cotangent, valid, dilation, band):
    ch, n = emb_rows.shape
    R, T = lax.axis_size("row"), lax.axis_size("diag")
    q, t = lax.axis_index("row"), lax.axis_index("diag")
    wide, ext, m = 2 * n, n + 2 * MAXDIL, MAXDIL
    bf, f32 = jnp.bfloat16, jnp.float32

    pack = jnp.concatenate(
        [emb_cols, emb_rows, jnp.broadcast_to(valid.astype(bf)[None], (16, n))], axis=0)
    every = lax.all_gather(pack, "row", axis=1, tiled=True)
    every = jnp.pad(every, ((0, 0), (n, n * (T + 2))))
    win = lax.dynamic_slice_in_dim(every, n * (q + t), 4 * n, 1)
    near = lax.dynamic_slice_in_dim(every, n * q, 3 * n, 1)[:, n - m : 2 * n + m]
    s = 28
    low = jnp.concatenate([win[:, n : n + wide - s], win[:, n - s : n]], axis=1)
    high = jnp.concatenate([win[:, n + wide : n + wide + s], win[:, n + s : n + wide]], axis=1)
    both = jnp.stack([low, high]).astype(f32)
    cols = both[:, :ch]
    vcol = both[:, 2 * ch : 2 * ch + RG]
    vr = near[2 * ch].astype(f32)
    rows = jnp.broadcast_to(near[ch : 2 * ch].T[:, :, None], (ext, ch, n))

    cot = jnp.transpose(cotangent, (1, 0, 2))
    before, after = with_halo(cot, "row", 0, m)
    cot = jnp.concatenate([before, cot, after], axis=0)
    before, after = with_halo(cot, "diag", 2, 2 * m)
    halo = jnp.concatenate([after, jnp.zeros((ext, ch, n - 4 * m), bf), before], axis=2)

    blk = RG * ch
    kf = jnp.tile(kernel.reshape(9, ch, ch), (1, 1, 2 * RG))
    kb = jnp.tile(jnp.swapaxes(kernel.reshape(9, ch, ch), 1, 2), (1, 1, 2 * RG))
    par = jnp.stack([dilation[0], band[0], (t * n).astype(jnp.int32)])
    bias2 = jnp.broadcast_to(bias[:, None], (ch, wide))
    nk = (9 * ch * ch) // (RG * 128) + 1
    vmem = pl.BlockSpec(memory_space=pltpu.VMEM)
    smem = pl.BlockSpec(memory_space=pltpu.SMEM)
    out, rsum, csum, kg = pl.pallas_call(
        pair_kernel,
        out_shape=(
            jax.ShapeDtypeStruct((n, ch, n), bf),
            jax.ShapeDtypeStruct((ch, n), f32),
            jax.ShapeDtypeStruct((ch, wide), f32),
            jax.ShapeDtypeStruct((nk, RG, 128), f32),
        ),
        in_specs=[smem, smem] + [vmem] * 8,
        out_specs=(vmem,) * 4,
        scratch_shapes=[
            pltpu.VMEM((3, ext * ch, wide), bf),
            pltpu.VMEM((3, ext * ch, wide), bf),
            pltpu.VMEM((ext * ch, wide), bf),
            pltpu.VMEM((ext * ch, wide), f32),
            pltpu.VMEM((ext * ch, wide), f32),
            pltpu.VMEM((3, blk, 2 * blk), bf),
            pltpu.VMEM((3, blk, 2 * blk), bf),
            pltpu.VMEM((3, blk, 2 * blk), f32),
            pltpu.VMEM((ch, wide), f32),
        ],
        compiler_params=pltpu.CompilerParams(vmem_limit_bytes=56 * 2**20),
        name="pair_kernel",
    )(par, vr, rows, cols, vcol, cot, halo, kf, kb, bias2)

    Z = ch // RG
    dma = pltpu.SemaphoreType.DMA
    tile = lambda *lead: pltpu.VMEM(lead + (RG, n), f32)
    kg, rc = pl.pallas_call(
        functools.partial(sum_kernel, R, T),
        out_shape=(
            jax.ShapeDtypeStruct((nk, RG, 128), f32),
            jax.ShapeDtypeStruct((Z, 2, RG, n), f32),
        ),
        in_specs=[vmem] * 3,
        out_specs=(vmem,) * 2,
        scratch_shapes=[
            tile(R * T), tile(T), tile(R), tile(R), tile(), tile(2), tile(nk), tile(Z, 2),
            dma((nk,)), dma((R * T,)), dma((Z,)), dma((T,)), dma((Z,)), dma((R,)), dma((Z,)), dma((R,)),
            dma((R * T,)), dma((nk,)), dma((T,)), dma((Z,)),
        ],
        compiler_params=pltpu.CompilerParams(collective_id=0, has_side_effects=True),
        name="sum_kernel",
    )(kg, rsum.reshape(Z, RG, n), csum.reshape(Z, RG, 2, n).transpose(2, 0, 1, 3))

    embed_scale = 1.0 / jnp.sqrt(jnp.float32(T * n))
    weight_scale = 1.0 / jnp.sqrt(jnp.float32(R * n) * jnp.float32(T * n))
    kgt = kg[:-1].reshape(-1, 4, ch).transpose(1, 0, 2).reshape(3, 3, ch, ch)
    bgt = kg[-1].reshape(RG, 4, ch)[:, :, 0].T.reshape(ch)
    return (
        jnp.transpose(out, (1, 0, 2)),
        rc[:, 0].reshape(ch, n) * embed_scale,
        rc[:, 1].reshape(ch, n) * embed_scale,
        kgt * weight_scale,
        bgt * weight_scale,
    )


def solution(mesh):
    in_specs = (
        P(None, ("grp", "row")),
        P(None, ("grp", "row")),
        P(),
        P(),
        P(None, ("grp", "row"), "diag"),
        P(("grp", "row")),
        P("grp"),
        P("grp"),
    )
    out_specs = (
        P(None, ("grp", "row"), "diag"),
        P(None, ("grp", "row")),
        P(None, ("grp", "row")),
        P("grp", None, None, None),
        P("grp"),
    )
    return jax.shard_map(local, mesh=mesh, in_specs=in_specs, out_specs=out_specs, check_vma=False)
```

profile of v0, /device:TPU:0, one launch (start us, length us, event | category | flops | bytes accessed | tf_op | source)
XLA Modules:
  0.0 96.9 jit_solution(15392745495886724162)
XLA Ops:
  0.7 1.9 %copy.50 = bf16[32,128,128]{2,0,1:T(8,128)(2,1)S(1)} copy(bf16[32,128,128]{2,1,0:T(8,128)(2,1)} %param.12) | data formatting | bytes 2097152 | tf_op args[4]
  2.6 0.0 copy-start.1
  2.6 2.4 %collective-permute-start = (bf16[4,32,128]{2,1,0:T(8,128)(2,1)S(1)}, bf16[4,32,128]{2,1,0:T(8,128)(2,1)S(1)}, u32[]{:S(2)}, u32[]{:S(2)}) collective-permute-start(bf16[4,32,128]{2,1,0:T(8,128)(2,1)S(1)} %get-tuple-element.39), channel_id=1, source_target_pairs={{0,4},{4,8},{8,12},{1,5},{5,9},{9,13},{2,6},{6,10},{10,14},{3,7},{... | collective-permute-start | bytes 98312 | tf_op jit(solution)/shard_map/ppermute | solution.py:22
  5.0 1.3 %collective-permute-start.1 = (bf16[4,32,128]{2,1,0:T(8,128)(2,1)S(1)}, bf16[4,32,128]{2,1,0:T(8,128)(2,1)S(1)}, u32[]{:S(2)}, u32[]{:S(2)}) collective-permute-start(bf16[4,32,128]{2,1,0:T(8,128)(2,1)S(1)} %get-tuple-element.40), channel_id=1, source_target_pairs={{4,0},{8,4},{12,8},{5,1},{9,5},{13,9},{6,2},{10,6},{14,10},{7,3},{... | collective-permute-start | bytes 98312 | tf_op jit(solution)/shard_map/ppermute | solution.py:22
  6.4 8.2 %all_gather.3 = bf16[80,512]{1,0:T(8,128)(2,1)S(1)} all-gather(bf16[80,128]{1,0:T(8,128)(2,1)S(1)} %pad_maximum_fusion.2), channel_id=1, replica_groups=mesh['grp'=2,'row'=4,'diag'=4] {'row'}, dimensions={1}, use_global_device_ids=true | all-gather | bytes 102400 | tf_op jit(solution)/shard_map/all_gather | solution.py:313
  14.6 0.1 pad_dynamic-slice_fusion.2
  14.7 0.1 pad_dynamic-slice_fusion.1
  14.8 0.1 maximum_bitcast_fusion
  14.9 0.6 fusion.1.vcol
  15.5 0.6 maximum_convert_fusion.cols
  16.2 0.1 fusion
  16.2 0.6 fusion.2
  16.9 0.1 copy.33
  18.3 0.1 copy.39
  18.4 0.2 tile.22
  18.6 1.9 %tile.23.kb = bf16[9,32,512]{2,1,0:T(8,128)(2,1)} reshape(bf16[9,32,16,32]{3,2,1,0:T(8,128)(2,1)S(1)} %tile.22) | data formatting | bytes 589824 | tf_op jit(solution)/shard_map/tile | solution.py:334
  20.4 0.2 tile.20
  20.6 1.9 %tile.21.kf = bf16[9,32,512]{2,1,0:T(8,128)(2,1)} reshape(bf16[9,32,16,32]{3,2,1,0:T(8,128)(2,1)S(1)} %tile.20) | data formatting | bytes 589824 | tf_op jit(solution)/shard_map/tile | solution.py:333
  22.5 0.1 pad.6.clone
  22.5 0.0 collective-permute-done
  22.5 0.0 collective-permute-done.1
  22.5 0.1 pad_maximum_fusion.cot
  22.7 0.5 fusion.3
  23.2 0.5 copy-done
  23.7 1.3 %copy.35 = bf16[136,32,8]{0,2,1:T(8,128)(2,1)S(1)} copy(bf16[136,32,8]{2,1,0:T(8,128)(2,1)S(1)} %get-tuple-element.37) | data formatting | bytes 139264 | tf_op jit(solution)/shard_map/slice | solution.py:21
  25.0 1.3 %collective-permute-start.2 = (bf16[136,32,8]{0,2,1:T(8,128)(2,1)S(1)}, bf16[136,32,8]{0,2,1:T(8,128)(2,1)S(1)}, u32[]{:S(2)}, u32[]{:S(2)}) collective-permute-start(bf16[136,32,8]{0,2,1:T(8,128)(2,1)S(1)} %copy.35), channel_id=1, source_target_pairs={{1,0},{2,1},{3,2},{5,4},{6,5},{7,6},{9,8},{10,9},{11,10},{13,12},{... | collective-permute-start | bytes 208904 | tf_op jit(solution)/shard_map/ppermute | solution.py:22
  26.3 1.3 %copy.36 = bf16[136,32,8]{0,2,1:T(8,128)(2,1)S(1)} copy(bf16[136,32,8]{2,1,0:T(8,128)(2,1)S(1)} %get-tuple-element.38) | data formatting | bytes 139264 | tf_op jit(solution)/shard_map/slice | solution.py:20
  27.7 4.7 %collective-permute-start.3 = (bf16[136,32,8]{0,2,1:T(8,128)(2,1)S(1)}, bf16[136,32,8]{0,2,1:T(8,128)(2,1)S(1)}, u32[]{:S(2)}, u32[]{:S(2)}) collective-permute-start(bf16[136,32,8]{0,2,1:T(8,128)(2,1)S(1)} %copy.36), channel_id=1, source_target_pairs={{0,1},{1,2},{2,3},{4,5},{5,6},{6,7},{8,9},{9,10},{10,11},{12,13},{... | collective-permute-start | bytes 208904 | tf_op jit(solution)/shard_map/ppermute | solution.py:22
  32.4 0.6 pad_add_fusion.par
  33.0 0.0 collective-permute-done.2
  33.0 1.5 %copy.37 = bf16[136,32,8]{2,1,0:T(8,128)(2,1)S(1)} copy(bf16[136,32,8]{0,2,1:T(8,128)(2,1)S(1)} %collective-permute-done.2) | data formatting | bytes 139264 | tf_op jit(solution)/shard_map/ppermute | solution.py:22
  34.5 0.6 collective-permute-done.3
  35.2 1.5 %copy.38 = bf16[136,32,8]{2,1,0:T(8,128)(2,1)S(1)} copy(bf16[136,32,8]{0,2,1:T(8,128)(2,1)S(1)} %collective-permute-done.3) | data formatting | bytes 139264 | tf_op jit(solution)/shard_map/ppermute | solution.py:22
  36.7 1.7 %pad_maximum_fusion.1.halo = bf16[136,32,128]{2,1,0:T(8,128)(2,1)} fusion(bf16[136,32,8]{2,1,0:T(8,128)(2,1)S(1)} %copy.38, bf16[136,32,8]{2,1,0:T(8,128)(2,1)S(1)} %copy.37, bf16[128]{0:T(256)(128)(2,1)S(1)} %pad.6.clone), kind=kLoop, calls=%fused_computation.1 | loop fusion | flops 3342336 | bytes 1253632 | tf_op jit(solution)/shard_map/concatenate | solution.py:330
  38.4 1.8 %broadcast_in_dim.9.rows = bf16[136,32,128]{2,1,0:T(8,128)(2,1)} broadcast(bf16[136,32]{1,0:T(8,128)(2,1)S(1)} %copy.33), dimensions={0,1} | broadcast | bytes 1122816 | tf_op jit(solution)/shard_map/broadcast_in_dim | solution.py:324
  40.2 0.7 broadcast_in_dim.11.bias
  40.9 30.8 %pair_kernel.1 = (bf16[128,32,128]{2,1,0:T(8,128)(2,1)}, f32[32,128]{1,0:T(8,128)}, f32[32,256]{1,0:T(8,128)}, f32[10,8,128]{2,1,0:T(8,128)}) custom-call(s32[3]{0:T(128)} %pad_add_fusion.par, f32[136]{0:T(256)} %bitcast.45, bf16[136,32,128]{2,1,0:T(8,128)(2,1)} %broadcast_in_dim.9.rows, f32[2,32,256]{2,1,0:T(8,128)} %maximum_convert_fusion.cols, ...), custom_call_target="tpu_custom_call" | custom-call | tf_op jit(solution)/shard_map/pair_kernel/pallas_call | solution.py:340
  71.7 1.4 %copy_bitcast_fusion.1.col = f32[2,4,8,128]{3,2,1,0:T(8,128)} fusion(f32[32,256]{1,0:T(8,128)} %get-tuple-element.14), kind=kLoop, calls=%fused_computation.13 | loop fusion | bytes 65536 | tf_op jit(solution)/shard_map/transpose | solution.py:383
  73.1 16.8 %sum_kernel.1 = (f32[10,8,128]{2,1,0:T(8,128)}, f32[4,2,8,128]{3,2,1,0:T(8,128)}) custom-call(f32[10,8,128]{2,1,0:T(8,128)} %get-tuple-element.12.kg, f32[4,8,128]{2,1,0:T(8,128)} %bitcast.44, f32[2,4,8,128]{3,2,1,0:T(8,128)} %copy_bitcast_fusion.1.col), custom_call_target="tpu_custom_call" | custom-call | tf_op jit(solution)/shard_map/sum_kernel/pallas_call | solution.py:368
  89.9 0.8 slice_multiply_fusion
  90.7 0.7 slice.69
  91.4 0.1 mul.60
  91.5 0.7 copy.45
  92.2 1.3 %multiply_bitcast_fusion = (f32[32,128]{1,0:T(8,128)}, f32[32,128]{1,0:T(8,128)}) fusion(f32[4,2,8,128]{3,2,1,0:T(8,128)} %get-tuple-element.15), kind=kLoop, calls=%fused_computation.15 | loop fusion | flops 8192 | bytes 65536 | tf_op jit(solution)/shard_map/mul | solution.py:392
  93.5 0.1 reshape_squeeze.2
  93.6 0.1 copy.47
  93.7 0.6 mul.67
  94.3 2.6 %copy.43 = bf16[32,128,128]{2,1,0:T(8,128)(2,1)} copy(bf16[32,128,128]{2,0,1:T(8,128)(2,1)} %bitcast.38) | data formatting | bytes 2097152
  (16 shorter events, 0.0 us)
Async XLA Ops:
  0.6 5.7 %copy-start.5 = (s32[128]{0:T(128)S(1)}, s32[128]{0:T(128)}, u32[]{:S(2)}) copy-start(s32[128]{0:T(128)} %param.13) | copy-start | bytes 1540
  0.6 5.7 %copy-start.2 = (bf16[32,128]{1,0:T(8,128)(2,1)S(1)}, bf16[32,128]{1,0:T(8,128)(2,1)}, u32[]{:S(2)}) copy-start(bf16[32,128]{1,0:T(8,128)(2,1)} %param.8) | copy-start | bytes 24580
  0.7 5.7 %copy-start.3 = (bf16[32,128]{1,0:T(8,128)(2,1)S(1)}, bf16[32,128]{1,0:T(8,128)(2,1)}, u32[]{:S(2)}) copy-start(bf16[32,128]{1,0:T(8,128)(2,1)} %param.9) | copy-start | bytes 24580
  2.6 15.7 %copy-start.1 = (bf16[3,3,32,32]{3,2,1,0:T(8,128)(2,1)S(1)}, bf16[3,3,32,32]{3,2,1,0:T(8,128)(2,1)}, u32[]{:S(2)}) copy-start(bf16[3,3,32,32]{3,2,1,0:T(8,128)(2,1)} %param.10) | copy-start | bytes 55300
  2.6 19.9 %collective-permute-start = (bf16[4,32,128]{2,1,0:T(8,128)(2,1)S(1)}, bf16[4,32,128]{2,1,0:T(8,128)(2,1)S(1)}, u32[]{:S(2)}, u32[]{:S(2)}) collective-permute-start(bf16[4,32,128]{2,1,0:T(8,128)(2,1)S(1)} %get-tuple-element.39), channel_id=1, source_target_pairs={{0,4},{4,8},{8,12},{1,5},{5,9},{9,13},{2,6},{6,10},{10,14},{3,7},{... | collective-permute-start | bytes 98312 | tf_op jit(solution)/shard_map/ppermute | solution.py:22
  5.0 17.5 %collective-permute-start.1 = (bf16[4,32,128]{2,1,0:T(8,128)(2,1)S(1)}, bf16[4,32,128]{2,1,0:T(8,128)(2,1)S(1)}, u32[]{:S(2)}, u32[]{:S(2)}) collective-permute-start(bf16[4,32,128]{2,1,0:T(8,128)(2,1)S(1)} %get-tuple-element.40), channel_id=1, source_target_pairs={{4,0},{8,4},{12,8},{5,1},{9,5},{13,9},{6,2},{10,6},{14,10},{7,3},{... | collective-permute-start | bytes 98312 | tf_op jit(solution)/shard_map/ppermute | solution.py:22
  22.7 1.0 %copy-start = (bf16[136,32,128]{2,1,0:T(8,128)(2,1)}, bf16[136,32,128]{2,1,0:T(8,128)(2,1)S(1)}, u32[]{:S(2)}) copy-start(bf16[136,32,128]{2,1,0:T(8,128)(2,1)S(1)} %pad_maximum_fusion.cot) | copy-start | bytes 3342340
  25.0 8.0 %collective-permute-start.2 = (bf16[136,32,8]{0,2,1:T(8,128)(2,1)S(1)}, bf16[136,32,8]{0,2,1:T(8,128)(2,1)S(1)}, u32[]{:S(2)}, u32[]{:S(2)}) collective-permute-start(bf16[136,32,8]{0,2,1:T(8,128)(2,1)S(1)} %copy.35), channel_id=1, source_target_pairs={{1,0},{2,1},{3,2},{5,4},{6,5},{7,6},{9,8},{10,9},{11,10},{13,12},{... | collective-permute-start | bytes 208904 | tf_op jit(solution)/shard_map/ppermute | solution.py:22
  27.7 7.5 %collective-permute-start.3 = (bf16[136,32,8]{0,2,1:T(8,128)(2,1)S(1)}, bf16[136,32,8]{0,2,1:T(8,128)(2,1)S(1)}, u32[]{:S(2)}, u32[]{:S(2)}) collective-permute-start(bf16[136,32,8]{0,2,1:T(8,128)(2,1)S(1)} %copy.36), channel_id=1, source_target_pairs={{0,1},{1,2},{2,3},{4,5},{5,6},{6,7},{8,9},{9,10},{10,11},{12,13},{... | collective-permute-start | bytes 208904 | tf_op jit(solution)/shard_map/ppermute | solution.py:22
  38.4 1.8 %copy-start.4 = (f32[32]{0:T(128)S(1)}, f32[32]{0:T(128)}, u32[]{:S(2)}) copy-start(f32[32]{0:T(128)} %param.11) | copy-start | bytes 388
where the time goes:
time: 97.5 us; the launch traced here: 96.9 us
  Pallas kernels  47.6 us (49%)
  local copies, waits for them, and re-layouts  22 us (23%)
  starting transfers between devices  9.7 us (10%)
  blocking collectives  8.2 us (8%)
  other arithmetic  6.55 us (7%)
  between operations  2.17 us (2%)
    pallas_call x1, Pallas kernels, local(): pl.pallas_call(pair_kernel, out_shape=(jax.ShapeDtypeStruct((n, ch, n), b...  30.8 us
    pallas_call x1, Pallas kernels, local(): pl.pallas_call(functools.partial(sum_kernel, R, T), out_shape=(jax.ShapeD...  16.8 us
    ppermute x4, starting transfers between devices, with_halo(): return (lax.ppermute(last, axis, up), lax.ppermute(initial, axis, down))  9.7 us
    all_gather x1, blocking collectives, local(): every = lax.all_gather(pack, 'row', axis=1, tiled=True)  8.2 us
    unnamed x16, local copies, waits for them, and re-layouts  5.8 us
    ppermute x2, local copies, waits for them, and re-layouts, with_halo(): return (lax.ppermute(last, axis, up), lax.ppermute(initial, axis, down))  3.03 us
    another operation x2, local copies, waits for them, and re-layouts, local(): kb = jnp.tile(jnp.swapaxes(kernel.reshape(9, ch, ch), 1, 2), (1, 1, 2 * RG))  2.02 us
    another operation x2, local copies, waits for them, and re-layouts, local(): kf = jnp.tile(kernel.reshape(9, ch, ch), (1, 1, 2 * RG))  2.01 us
  transfers between devices with their start and end apart: 4, of which 1 were waited for; matrix products, arithmetic and copies ran while one was open for 10% of the time, Pallas kernels for 0%

commit v1 on v0

--- a/solution.py
+++ b/solution.py
@@ -13,24 +13,178 @@
 CUBIC = 0.044715
 
 
-def with_halo(array, axis, dim, width):
-    size, length = (lax.axis_size(axis), array.shape[dim])
-    up = [(i, i + 1) for i in range(size - 1)]
-    down = [(j, i) for i, j in up]
-    last = lax.slice_in_dim(array, length - width, length, axis=dim)
-    initial = lax.slice_in_dim(array, 0, width, axis=dim)
-    return lax.ppermute(last, axis, up), lax.ppermute(initial, axis, down)
+def loop(count, body):
+    def step(p, c):
+        body(p)
+        return c
+    lax.fori_loop(0, count, step, 0)
+
+
+def send(src, dst, ss, sr, dq, dt):
+    return pltpu.make_async_remote_copy(
+        src_ref=src, dst_ref=dst, send_sem=ss, recv_sem=sr,
+        device_id={"row": dq, "diag": dt}, device_id_type=pl.DeviceIdType.MESH,
+    )
+
+
+def gather_kernel(
+    R, T, pack, cot, cols, vcol, near, ext, halo,
+    blocks, edge_l, edge_r, from_r, from_l, top, bottom,
+    ps, pr, hs, hr,
+):
+    n, ch = cot.shape[0], cot.shape[1]
+    m = MAXDIL
+    width = 2 * m
+    per = n // width
+    tiles = n // per
+    q, t = lax.axis_index("row"), lax.axis_index("diag")
+    bf, f32 = jnp.bfloat16, jnp.float32
+    mesh_id = pl.DeviceIdType.MESH
+    barrier = pltpu.get_barrier_semaphore()
+    left, right, above, below = t > 0, t < T - 1, q > 0, q < R - 1
+
+    def greet(p):
+        @pl.when(p != q)
+        def _():
+            pl.semaphore_signal(barrier, inc=1, device_id={"row": p, "diag": t}, device_id_type=mesh_id)
+    loop(R, greet)
+    sides = []
+    for dt, okt in ((-1, left), (1, right)):
+        for dq, okq in ((-1, above), (0, True), (1, below)):
+            sides.append((dq, dt, okt & okq))
+    total = R - 1
+    for dq, dt, ok in sides:
+        total = total + jnp.where(ok, 1, 0)
+
+        @pl.when(ok)
+        def _():
+            pl.semaphore_signal(barrier, inc=1, device_id={"row": q + dq, "diag": t + dt}, device_id_type=mesh_id)
+
+    lane = lax.broadcasted_iota(jnp.int32, (ch, n), 1)
+
+    def pack_edges(g):
+        a = jnp.zeros((ch, n), f32)
+        b = jnp.zeros((ch, n), f32)
+        for s in range(per):
+            x = cot[g * per + s].astype(f32)
+            here = lane // width == s
+            a = jnp.where(here, pltpu.roll(x, width * s, 1) if s else x, a)
+            sh = (width * (s + 1)) % n
+            b = jnp.where(here, pltpu.roll(x, sh, 1) if sh else x, b)
+        edge_l[g] = a.astype(bf)
+        edge_r[g] = b.astype(bf)
+    loop(tiles, pack_edges)
+    pl.semaphore_wait(barrier, total)
+
+    def p1(p):
+        return send(pack, blocks.at[q + 1], ps.at[p], pr.at[q], p, t)
+
+    def halos(act):
+        last = tiles - 1
+        plan = (
+            (left, edge_l, from_r.at[pl.ds(0, tiles)], 0, 0, -1),
+            (right, edge_r, from_l.at[pl.ds(0, tiles)], 1, 0, 1),
+            (above, cot.at[pl.ds(0, m)], bottom, 2, -1, 0),
+            (below, cot.at[pl.ds(n - m, m)], top, 3, 1, 0),
+            (below & left, edge_l.at[last], from_r.at[tiles], 4, 1, -1),
+            (above & left, edge_l.at[0], from_r.at[tiles + 1], 5, -1, -1),
+            (below & right, edge_r.at[last], from_l.at[tiles], 6, 1, 1),
+            (above & right, edge_r.at[0], from_l.at[tiles + 1], 7, -1, 1),
+        )
+        flags = {(0, -1): right, (0, 1): left, (-1, 0): below, (1, 0): above,
+                 (1, -1): above & right, (-1, -1): below & right, (1, 1): above & left, (-1, 1): below & left}
+        for ok, src, dst, k, dq, dt in plan:
+            act(ok, flags[(dq, dt)], src, dst, send(src, dst, hs.at[k], hr.at[k], q + dq, t + dt))
+
+    def start(ok, got, src, dst, c):
+        @pl.when(ok)
+        def _():
+            c.start()
+
+    def peers(act):
+        def one(p):
+            @pl.when(p != q)
+            def _():
+                act(p)
+        loop(R, one)
+
+    peers(lambda p: p1(p).start())
+    halos(start)
+
+    zero = jnp.zeros(pack.shape, bf)
+    blocks[0] = zero
+    for k in range(R + 1, R + T + 3):
+        blocks[k] = zero
+    blocks[q + 1] = pack[...]
+
+    def body_copy(g):
+        for s in range(RG):
+            ext[m + g * RG + s] = cot[g * RG + s]
+    loop(n // RG, body_copy)
+
+    peers(lambda p: send(pack, blocks.at[p + 1], ps.at[p], pr.at[p], q, t).wait_recv())
+    rows_of = slice(ch, 2 * ch + RG)
+    lane2 = lax.broadcasted_iota(jnp.int32, pack.shape, 1)
+    b0, b1, b2, b3 = (blocks[q + t + k].astype(f32) for k in range(4))
+    s = 28
+    low = (b1, jnp.where(lane2 >= n - s, b0, b2))
+    high = (jnp.where(lane2 < s, b3, b1), b2)
+    for side, (x, y) in enumerate((low, high)):
+        cols[side, :, :n] = x[:ch]
+        cols[side, :, n:] = y[:ch]
+        vcol[side, :, :n] = x[2 * ch : 2 * ch + RG]
+        vcol[side, :, n:] = y[2 * ch : 2 * ch + RG]
+    near[0] = blocks[q + 1].astype(f32)[rows_of]
+    near[1] = jnp.where(lane2 >= n - m, blocks[q].astype(f32), blocks[q + 2].astype(f32))[rows_of]
+
+    def finish(ok, got, src, dst, c):
+        @pl.when(got)
+        def _():
+            c.wait_recv()
+
+        @pl.when(jnp.logical_not(got))
+        def _():
+            dst[...] = jnp.zeros(dst.shape, bf)
+    halos(finish)
+    for s in range(m):
+        ext[s] = top[s]
+        ext[n + m + s] = bottom[s]
+
+    def spread(e, tile_r, tile_l, s):
+        a = pltpu.roll(tile_r, (n - width * s) % n, 1) if s else tile_r
+        b = pltpu.roll(tile_l, (2 * n - width - width * s) % n, 1) if (n - width - width * s) % n else tile_l
+        halo[e] = jnp.where(lane < width, a, jnp.where(lane >= n - width, b, 0.0)).astype(bf)
+
+    def unpack(g):
+        tr, tl = from_r[g].astype(f32), from_l[g].astype(f32)
+        for s in range(per):
+            spread(m + g * per + s, tr, tl, s)
+    loop(tiles, unpack)
+    tr, tl = from_r[tiles].astype(f32), from_l[tiles].astype(f32)
+    for s in range(m):
+        spread(s, tr, tl, per - m + s)
+    tr, tl = from_r[tiles + 1].astype(f32), from_l[tiles + 1].astype(f32)
+    for s in range(m):
+        spread(n + m + s, tr, tl, s)
+
+    peers(lambda p: p1(p).wait_send())
+
+    def sent(ok, got, src, dst, c):
+        @pl.when(ok)
+        def _():
+            c.wait_send()
+    halos(sent)
 
 
 def pair_kernel(
-    par, vr, rows, cols, vcol, cot, halo, kf, kb, bias,
-    out, rsum, csum, kgrad,
-    act3, gz3, gzm, hid, der, tf, tb, kacc, bacc,
+    dilation, band, near, cols, vcol, cot, halo, kf, kb, bias,
+    out, rout, cout, kgrad,
+    act3, gz3, gzm, hid, der, tf, tb, kacc, bacc, rsum, csum,
 ):
     n = out.shape[0]
     ch = out.shape[1]
     wide = 2 * n
-    r, w, d0 = par[0], par[1], par[2]
+    r, w, d0 = dilation[0], band[0], lax.axis_index("diag") * n
     groups = n // RG
     blk = RG * ch
     lane1 = lax.broadcasted_iota(jnp.int32, (RG, wide), 1)
@@ -40,20 +194,26 @@
         d = jnp.where(d < -(n // 2), d + wide, d)
         return jnp.where(d >= wide - n // 2, d - wide, d)
 
-    def validity(e, i, side):
+    def at_row(i, first, size):
+        half = jnp.where((i < 0) | (i >= n), 1, 0)
+        x = pltpu.roll(near[half, first : first + size, :], lax.rem(2 * n - i, n), 1)
+        return jnp.broadcast_to(x[:, :1], (size, wide))
+
+    def validity(i, side):
         d = offsets(i)
         inside = (d + d0 >= 0) & (d + d0 < w)
-        v = jnp.where(inside, vcol[side] * vr[e], 0.0)
+        v = jnp.where(inside, vcol[side] * at_row(i, ch, RG), 0.0)
         return v, d
 
+    reps = 2 * blk // kf.shape[2]
     kblk = lax.broadcasted_iota(jnp.int32, (ch, 2 * blk), 1) // ch
     for b in range(3):
         for ii in range(RG):
             f = jnp.zeros((ch, 2 * blk), jnp.float32)
             g = jnp.zeros((ch, 2 * blk), jnp.float32)
             for a in range(3):
-                f = jnp.where(kblk == ii + MAXDIL + (a - 1) * r, kf[3 * a + b].astype(jnp.float32), f)
-                g = jnp.where(kblk == ii + MAXDIL - (a - 1) * r, kb[3 * a + b].astype(jnp.float32), g)
+                f = jnp.where(kblk == ii + MAXDIL + (a - 1) * r, jnp.concatenate([kf[3 * a + b].astype(jnp.float32)] * reps, axis=1), f)
+                g = jnp.where(kblk == ii + MAXDIL - (a - 1) * r, jnp.concatenate([kb[3 * a + b].astype(jnp.float32)] * reps, axis=1), g)
             tf[b, ii * ch : (ii + 1) * ch, :] = f.astype(jnp.bfloat16)
             tb[b, ii * ch : (ii + 1) * ch, :] = g.astype(jnp.bfloat16)
 
@@ -62,11 +222,10 @@
         for ii in range(RG):
             e = gi * RG + ii
             i = e - MAXDIL
-            v8, d8 = validity(e, i, side)
+            v8, d8 = validity(i, side)
             v = jnp.concatenate([v8] * (ch // RG), axis=0)
             d = jnp.concatenate([d8] * (ch // RG), axis=0)
-            rw = rows[e].astype(jnp.float32)
-            h = (jnp.concatenate([rw, rw], axis=1) + cols[side]) * v
+            h = (at_row(i, 0, ch) + cols[side]) * v
             h2 = h * h
             t = jnp.tanh(S2PI * h * (1.0 + CUBIC * h2))
             cdf = 0.5 * (1.0 + t)
@@ -113,7 +272,7 @@
         for ii in range(RG):
             i = gi * RG + ii
             side = jnp.where(i + MAXDIL >= (n // 2 // RG) * RG + RG, 1, 0)
-            v8, _ = validity(i + MAXDIL, i, side)
+            v8, _ = validity(i, side)
             v = jnp.concatenate([v8] * (ch // RG), axis=0)
             sl = slice(ii * ch, (ii + 1) * ch)
             po = (hz[sl] + bias[...]) * v
@@ -129,6 +288,10 @@
 
     lax.fori_loop(0, groups, phase_b, 0)
 
+    for z in range(ch // RG):
+        rout[z] = rsum[z * RG : (z + 1) * RG, :]
+        for k in range(2):
+            cout[k, z] = csum[z * RG : (z + 1) * RG, k * n : (k + 1) * n]
     lanes = lax.broadcasted_iota(jnp.int32, (RG, 128), 1) // ch
     pieces = []
     for a in range(3):
@@ -156,7 +319,7 @@
 
 
 def sum_kernel(
-    R, T, kg, row, col, kg_out, rc_out,
+    R, T, embed_scale, weight_scale, kg, row, col, kg_out, row_out, col_out,
     kbuf, rbuf, abuf, bbuf, ksum, rcsum, kres, rcres,
     ks, kr, rs, rr, as_, ar, bs, br, k2s, k2r, r2s, r2r,
 ):
@@ -165,18 +328,6 @@
     q, t = lax.axis_index("row"), lax.axis_index("diag")
     me = q * T + t
 
-    def loop(count, body):
-        def step(p, c):
-            body(p)
-            return c
-        lax.fori_loop(0, count, step, 0)
-
-    def send(src, dst, ss, sr, dq, dt):
-        return pltpu.make_async_remote_copy(
-            src_ref=src, dst_ref=dst, send_sem=ss, recv_sem=sr,
-            device_id={"row": dq, "diag": dt}, device_id_type=pl.DeviceIdType.MESH,
-        )
-
     barrier = pltpu.get_barrier_semaphore()
 
     def greet(p):
@@ -255,6 +406,7 @@
                 got(kbuf.at[p], kr.at[p])
                 ksum[...] += kbuf[p]
         loop(N, take)
+        ksum[...] = ksum[...] * weight_scale
         kres[me] = ksum[...]
 
     @pl.when(t < Z)
@@ -284,6 +436,7 @@
                 got(bbuf.at[p], br.at[p])
                 rcsum[1] += bbuf[p]
         loop(R, take_col)
+        rcsum[...] = rcsum[...] * embed_scale
         rcres[t] = rcsum[...]
 
     second(lambda c: c.start())
@@ -296,7 +449,9 @@
         def _():
             got(rcres.at[z], r2r.at[z])
     kg_out[...] = kres[...]
-    rc_out[...] = rcres[...]
+    for z in range(Z):
+        row_out[z * RG : (z + 1) * RG, :] = rcres[z, 0]
+        col_out[z * RG : (z + 1) * RG, :] = rcres[z, 1]
     first(lambda c: c.wait_send())
     second(lambda c: c.wait_send())
 
@@ -304,45 +459,49 @@
 def local(emb_rows, emb_cols, kernel, bias, cotangent, valid, dilation, band):
     ch, n = emb_rows.shape
     R, T = lax.axis_size("row"), lax.axis_size("diag")
-    q, t = lax.axis_index("row"), lax.axis_index("diag")
     wide, ext, m = 2 * n, n + 2 * MAXDIL, MAXDIL
     bf, f32 = jnp.bfloat16, jnp.float32
 
     pack = jnp.concatenate(
         [emb_cols, emb_rows, jnp.broadcast_to(valid.astype(bf)[None], (16, n))], axis=0)
-    every = lax.all_gather(pack, "row", axis=1, tiled=True)
-    every = jnp.pad(every, ((0, 0), (n, n * (T + 2))))
-    win = lax.dynamic_slice_in_dim(every, n * (q + t), 4 * n, 1)
-    near = lax.dynamic_slice_in_dim(every, n * q, 3 * n, 1)[:, n - m : 2 * n + m]
-    s = 28
-    low = jnp.concatenate([win[:, n : n + wide - s], win[:, n - s : n]], axis=1)
-    high = jnp.concatenate([win[:, n + wide : n + wide + s], win[:, n + s : n + wide]], axis=1)
-    both = jnp.stack([low, high]).astype(f32)
-    cols = both[:, :ch]
-    vcol = both[:, 2 * ch : 2 * ch + RG]
-    vr = near[2 * ch].astype(f32)
-    rows = jnp.broadcast_to(near[ch : 2 * ch].T[:, :, None], (ext, ch, n))
-
     cot = jnp.transpose(cotangent, (1, 0, 2))
-    before, after = with_halo(cot, "row", 0, m)
-    cot = jnp.concatenate([before, cot, after], axis=0)
-    before, after = with_halo(cot, "diag", 2, 2 * m)
-    halo = jnp.concatenate([after, jnp.zeros((ext, ch, n - 4 * m), bf), before], axis=2)
+    vmem = pl.BlockSpec(memory_space=pltpu.VMEM)
+    smem = pl.BlockSpec(memory_space=pltpu.SMEM)
+    dma = pltpu.SemaphoreType.DMA
+    tiles = 2 * m
+    edges = lambda k: pltpu.VMEM((k, ch, n), bf)
+    cols, vcol, near, cot, halo = pl.pallas_call(
+        functools.partial(gather_kernel, R, T),
+        out_shape=(
+            jax.ShapeDtypeStruct((2, ch, wide), f32),
+            jax.ShapeDtypeStruct((2, RG, wide), f32),
+            jax.ShapeDtypeStruct((2, ch + RG, n), f32),
+            jax.ShapeDtypeStruct((ext, ch, n), bf),
+            jax.ShapeDtypeStruct((ext, ch, n), bf),
+        ),
+        in_specs=[vmem] * 2,
+        out_specs=(vmem,) * 5,
+        scratch_shapes=[
+            pltpu.VMEM((R + T + 3,) + pack.shape, bf),
+            edges(tiles), edges(tiles), edges(tiles + 2), edges(tiles + 2), edges(m), edges(m),
+            dma((R,)), dma((R,)), dma((8,)), dma((8,)),
+        ],
+        compiler_params=pltpu.CompilerParams(collective_id=1, has_side_effects=True),
+        name="gather_kernel",
+    )(pack, cot)
 
     blk = RG * ch
-    kf = jnp.tile(kernel.reshape(9, ch, ch), (1, 1, 2 * RG))
-    kb = jnp.tile(jnp.swapaxes(kernel.reshape(9, ch, ch), 1, 2), (1, 1, 2 * RG))
-    par = jnp.stack([dilation[0], band[0], (t * n).astype(jnp.int32)])
+    kf = jnp.tile(kernel.reshape(9, ch, ch), (1, 1, 4))
+    kb = jnp.tile(jnp.swapaxes(kernel.reshape(9, ch, ch), 1, 2), (1, 1, 4))
     bias2 = jnp.broadcast_to(bias[:, None], (ch, wide))
     nk = (9 * ch * ch) // (RG * 128) + 1
-    vmem = pl.BlockSpec(memory_space=pltpu.VMEM)
-    smem = pl.BlockSpec(memory_space=pltpu.SMEM)
+    Z = ch // RG
     out, rsum, csum, kg = pl.pallas_call(
         pair_kernel,
         out_shape=(
             jax.ShapeDtypeStruct((n, ch, n), bf),
-            jax.ShapeDtypeStruct((ch, n), f32),
-            jax.ShapeDtypeStruct((ch, wide), f32),
+            jax.ShapeDtypeStruct((Z, RG, n), f32),
+            jax.ShapeDtypeStruct((2, Z, RG, n), f32),
             jax.ShapeDtypeStruct((nk, RG, 128), f32),
         ),
         in_specs=[smem, smem] + [vmem] * 8,
@@ -357,22 +516,25 @@
             pltpu.VMEM((3, blk, 2 * blk), bf),
             pltpu.VMEM((3, blk, 2 * blk), f32),
             pltpu.VMEM((ch, wide), f32),
+            pltpu.VMEM((ch, n), f32),
+            pltpu.VMEM((ch, wide), f32),
         ],
         compiler_params=pltpu.CompilerParams(vmem_limit_bytes=56 * 2**20),
         name="pair_kernel",
-    )(par, vr, rows, cols, vcol, cot, halo, kf, kb, bias2)
-
-    Z = ch // RG
-    dma = pltpu.SemaphoreType.DMA
+    )(dilation, band, near, cols, vcol, cot, halo, kf, kb, bias2)
+
     tile = lambda *lead: pltpu.VMEM(lead + (RG, n), f32)
-    kg, rc = pl.pallas_call(
-        functools.partial(sum_kernel, R, T),
+    embed_scale = float(T * n) ** -0.5
+    weight_scale = float(R * n * T * n) ** -0.5
+    kg, row_grad, col_grad = pl.pallas_call(
+        functools.partial(sum_kernel, R, T, embed_scale, weight_scale),
         out_shape=(
             jax.ShapeDtypeStruct((nk, RG, 128), f32),
-            jax.ShapeDtypeStruct((Z, 2, RG, n), f32),
+            jax.ShapeDtypeStruct((ch, n), f32),
+            jax.ShapeDtypeStruct((ch, n), f32),
         ),
         in_specs=[vmem] * 3,
-        out_specs=(vmem,) * 2,
+        out_specs=(vmem,) * 3,
         scratch_shapes=[
             tile(R * T), tile(T), tile(R), tile(R), tile(), tile(2), tile(nk), tile(Z, 2),
             dma((nk,)), dma((R * T,)), dma((Z,)), dma((T,)), dma((Z,)), dma((R,)), dma((Z,)), dma((R,)),
@@ -380,18 +542,16 @@
         ],
         compiler_params=pltpu.CompilerParams(collective_id=0, has_side_effects=True),
         name="sum_kernel",
-    )(kg, rsum.reshape(Z, RG, n), csum.reshape(Z, RG, 2, n).transpose(2, 0, 1, 3))
-
-    embed_scale = 1.0 / jnp.sqrt(jnp.float32(T * n))
-    weight_scale = 1.0 / jnp.sqrt(jnp.float32(R * n) * jnp.float32(T * n))
+    )(kg, rsum, csum)
+
     kgt = kg[:-1].reshape(-1, 4, ch).transpose(1, 0, 2).reshape(3, 3, ch, ch)
     bgt = kg[-1].reshape(RG, 4, ch)[:, :, 0].T.reshape(ch)
     return (
         jnp.transpose(out, (1, 0, 2)),
-        rc[:, 0].reshape(ch, n) * embed_scale,
-        rc[:, 1].reshape(ch, n) * embed_scale,
-        kgt * weight_scale,
-        bgt * weight_scale,
+        row_grad,
+        col_grad,
+        kgt,
+        bgt,
     )
 
 

time: 97.5 us -> 82.3 us (0.84)
  Pallas kernels: 47.6 us -> 62.7 us
  starting transfers between devices: 9.7 us -> 0 us
  blocking collectives: 8.2 us -> 0 us
  local copies, waits for them, and re-layouts: 22 us -> 14.9 us
  other arithmetic: 6.55 us -> 1.99 us
    ppermute x4 -> x0, starting transfers between devices: 9.7 us -> none  [with_halo(): return (lax.ppermute(last, axis, up), lax.ppermute(initial, axis, down))]
    pallas_call x1 -> x2, Pallas kernels: 16.8 us -> 26.1 us  [the longest x1 14.2 us: local(): pl.pallas_call(functools.partial(sum_kernel, R, T, embed_scale, weight_sc...]
    all_gather x1 -> x0, blocking collectives: 8.2 us -> none  [local(): every = lax.all_gather(pack, 'row', axis=1, tiled=True)]
    pallas_call x1, Pallas kernels: 30.8 us -> 36.6 us  [local(): pl.pallas_call(pair_kernel, out_shape=(jax.ShapeDtypeStruct((n, ch, n), b...]
    ppermute x2 -> x0, local copies, waits for them, and re-layouts: 3.03 us -> none  [with_halo(): return (lax.ppermute(last, axis, up), lax.ppermute(initial, axis, down))]
    slice x6 -> x1, local copies, waits for them, and re-layouts: 3.4 us -> 0.77 us  [local(): kgt = kg[:-1].reshape(-1, 4, ch).transpose(1, 0, 2).reshape(3, 3, ch, ch)]
    mul x3 -> x0, other arithmetic: 2.13 us -> none  [the longest x1 1.35 us: local(): rc[:, 1].reshape(ch, n) * embed_scale]
    unnamed x16 -> x8, local copies, waits for them, and re-layouts: 5.8 us -> 7.68 us
  transfers between devices with their start and end apart: 4 -> 0, of which waited for: 1 -> 0; matrix products, arithmetic and copies ran while one was open for 10% -> 0% of each run, Pallas kernels for 0% -> 0%
where the time goes in v1:
time: 82.3 us; the launch traced here: 81.7 us
  Pallas kernels  62.7 us (76%)
  local copies, waits for them, and re-layouts  14.9 us (18%)
  between operations  2.07 us (3%)
  other arithmetic  1.99 us (2%)
    pallas_call x1, Pallas kernels, local(): pl.pallas_call(pair_kernel, out_shape=(jax.ShapeDtypeStruct((n, ch, n), b...  36.6 us
    pallas_call x1, Pallas kernels, local(): pl.pallas_call(functools.partial(sum_kernel, R, T, embed_scale, weight_sc...  14.2 us
    pallas_call x1, Pallas kernels, local(): pl.pallas_call(functools.partial(gather_kernel, R, T), out_shape=(jax.Sha...  11.9 us
    unnamed x8, local copies, waits for them, and re-layouts  7.68 us
    another operation x2, local copies, waits for them, and re-layouts, local(): kf = jnp.tile(kernel.reshape(9, ch, ch), (1, 1, 4))  1.79 us

profile of v1, /device:TPU:0, one launch (start us, length us, event | category | flops | bytes accessed | tf_op | source)
XLA Modules:
  0.0 81.7 jit_solution(12637331326000725968)
XLA Ops:
  0.6 0.0 copy-start
  2.0 0.7 convert_element_type.3
  2.7 1.3 %pad_maximum_fusion.pack = bf16[80,128]{1,0:T(8,128)(2,1)} fusion(bf16[16,128]{1,0:T(8,128)(2,1)S(1)} %broadcast_in_dim.4, bf16[32,128]{1,0:T(8,128)(2,1)} %param.8, bf16[32,128]{1,0:T(8,128)(2,1)} %param.9), kind=kLoop, calls=%fused_computation.1 | loop fusion | flops 61440 | bytes 40960 | tf_op jit(solution)/shard_map/concatenate | solution.py:465
  4.0 1.3 %broadcast_in_dim.5.bias = f32[32,256]{1,0:T(8,128)} broadcast(f32[32]{0:T(128)} %param.11), dimensions={0} | broadcast | bytes 32896 | tf_op jit(solution)/shard_map/broadcast_in_dim | solution.py:496
  5.3 1.0 %copy.23 = bf16[9,32,32]{2,1,0:T(8,128)(2,1)S(1)} copy(bf16[9,32,32]{1,2,0:T(8,128)(2,1)} %bitcast.16) | data formatting | bytes 36864 | tf_op jit(solution)/shard_map/transpose | solution.py:495
  6.3 0.1 tile.22
  6.4 0.8 tile.23.kb
  7.2 1.0 %tile.20 = bf16[9,32,4,32]{3,2,1,0:T(4,128)(2,1)S(1)} broadcast(bf16[9,32,32]{2,1,0:T(8,128)(2,1)} %bitcast.17), dimensions={0,1,3} | broadcast | bytes 92160 | tf_op jit(solution)/shard_map/tile | solution.py:494
  8.2 0.8 %tile.21.kf = bf16[9,32,128]{2,1,0:T(8,128)(2,1)} reshape(bf16[9,32,4,32]{3,2,1,0:T(4,128)(2,1)S(1)} %tile.20) | data formatting | bytes 147456 | tf_op jit(solution)/shard_map/tile | solution.py:494
  9.0 0.0 copy-done
  9.0 1.6 %copy.32 = bf16[32,128,128]{2,0,1:T(8,128)(2,1)} copy(bf16[32,128,128]{2,1,0:T(8,128)(2,1)S(1)} %copy-done) | data formatting | bytes 2097152 | tf_op args[4]
  10.7 11.9 %gather_kernel.1 = (f32[2,32,256]{2,1,0:T(8,128)}, f32[2,8,256]{2,1,0:T(8,128)}, f32[2,40,128]{2,1,0:T(8,128)}, bf16[136,32,128]{2,1,0:T(8,128)(2,1)}, bf16[136,32,128]{2,1,0:T(8,128)(2,1)}) custom-call(bf16[80,128]{1,0:T(8,128)(2,1)} %pad_maximum_fusion.pack, bf16[128,32,128]{2,1,0:T(8,128)(2,1)} %bitcast.13), custom_call_target="tpu_custom_call" | custom-call | tf_op jit(solution)/shard_map/gather_kernel/pallas_call | solution.py:473
  22.6 36.6 %pair_kernel.1 = (bf16[128,32,128]{2,1,0:T(8,128)(2,1)}, f32[4,8,128]{2,1,0:T(8,128)}, f32[2,4,8,128]{3,2,1,0:T(8,128)}, f32[10,8,128]{2,1,0:T(8,128)}) custom-call(s32[1]{0:T(128)S(6)} %copy.35.dilation, s32[1]{0:T(128)S(6)} %copy.36.band, f32[2,40,128]{2,1,0:T(8,128)} %get-tuple-element.17.near, f32[2,32,256]{2,1,0:T(8,128)} %get-tuple-element.18.cols, ...), custom_call_target="tpu_custom_call" | custom-call | tf_op jit(solution)/shard_map/pair_kernel/pallas_call | solution.py:499
  59.2 2.6 %copy.26 = bf16[32,128,128]{2,1,0:T(8,128)(2,1)} copy(bf16[32,128,128]{2,0,1:T(8,128)(2,1)} %bitcast.14) | data formatting | bytes 2097152
  61.8 14.2 %sum_kernel.1 = (f32[10,8,128]{2,1,0:T(8,128)}, f32[32,128]{1,0:T(8,128)}, f32[32,128]{1,0:T(8,128)}) custom-call(f32[10,8,128]{2,1,0:T(8,128)} %get-tuple-element.23.kg, f32[4,8,128]{2,1,0:T(8,128)} %get-tuple-element.24.row, f32[2,4,8,128]{3,2,1,0:T(8,128)} %get-tuple-element.25.col), custom_call_target="tpu_custom_call" | custom-call | tf_op jit(solution)/shard_map/sum_kernel/pallas_call | solution.py:529
  76.0 0.7 slice.10
  76.7 0.8 slice.9
  77.4 0.1 reshape_squeeze.3
  77.5 0.1 copy.30
  77.6 0.6 reshape.32
  78.2 0.1 reshape.30
  78.4 0.7 copy.28
  79.0 1.3 %copy.37 = f32[32,128]{1,0:T(8,128)} copy(f32[32,128]{1,0:T(8,128)} %get-tuple-element.50) | data formatting | bytes 32768
  80.3 1.3 %copy.38 = f32[32,128]{1,0:T(8,128)} copy(f32[32,128]{1,0:T(8,128)} %get-tuple-element.51) | data formatting | bytes 32768
  (1 shorter events, 0.0 us)
Async XLA Ops:
  0.6 8.4 %copy-start = (bf16[32,128,128]{2,1,0:T(8,128)(2,1)S(1)}, bf16[32,128,128]{2,1,0:T(8,128)(2,1)}, u32[]{:S(2)}) copy-start(bf16[32,128,128]{2,1,0:T(8,128)(2,1)} %param.12) | copy-start | bytes 3145732

commit v2 on v1

--- a/solution.py
+++ b/solution.py
@@ -177,9 +177,9 @@
 
 
 def pair_kernel(
-    dilation, band, near, cols, vcol, cot, halo, kf, kb, bias,
+    dilation, band, near, cols, vcol, cot, halo, kf, bias,
     out, rout, cout, kgrad,
-    act3, gz3, gzm, hid, der, tf, tb, kacc, bacc, rsum, csum,
+    act3, gz3, gzm, hid, der, tf, tb, kacc, bacc, rsum, csum, vbuf,
 ):
     n = out.shape[0]
     ch = out.shape[1]
@@ -205,15 +205,19 @@
         v = jnp.where(inside, vcol[side] * at_row(i, ch, RG), 0.0)
         return v, d
 
-    reps = 2 * blk // kf.shape[2]
+    def tiled(x):
+        return jnp.concatenate([jnp.concatenate([x] * 4, axis=1)] * (2 * blk // (4 * ch)), axis=1)
+
     kblk = lax.broadcasted_iota(jnp.int32, (ch, 2 * blk), 1) // ch
     for b in range(3):
+        fw = [tiled(kf[3 * a + b].astype(jnp.float32)) for a in range(3)]
+        bw = [tiled(kf[3 * a + b].astype(jnp.float32).T) for a in range(3)]
         for ii in range(RG):
             f = jnp.zeros((ch, 2 * blk), jnp.float32)
             g = jnp.zeros((ch, 2 * blk), jnp.float32)
             for a in range(3):
-                f = jnp.where(kblk == ii + MAXDIL + (a - 1) * r, jnp.concatenate([kf[3 * a + b].astype(jnp.float32)] * reps, axis=1), f)
-                g = jnp.where(kblk == ii + MAXDIL - (a - 1) * r, jnp.concatenate([kb[3 * a + b].astype(jnp.float32)] * reps, axis=1), g)
+                f = jnp.where(kblk == ii + MAXDIL + (a - 1) * r, fw[a], f)
+                g = jnp.where(kblk == ii + MAXDIL - (a - 1) * r, bw[a], g)
             tf[b, ii * ch : (ii + 1) * ch, :] = f.astype(jnp.bfloat16)
             tb[b, ii * ch : (ii + 1) * ch, :] = g.astype(jnp.bfloat16)
 
@@ -223,6 +227,7 @@
             e = gi * RG + ii
             i = e - MAXDIL
             v8, d8 = validity(i, side)
+            vbuf[e] = v8
             v = jnp.concatenate([v8] * (ch // RG), axis=0)
             d = jnp.concatenate([d8] * (ch // RG), axis=0)
             h = (at_row(i, 0, ch) + cols[side]) * v
@@ -254,6 +259,8 @@
     csum[...] = jnp.zeros_like(csum)
     lane_n = lax.broadcasted_iota(jnp.int32, (ch, n), 1)
 
+    bias_all = jnp.broadcast_to(bias[...], (ch, wide))
+
     def phase_b(gi, carry):
         big = pl.ds(pl.multiple_of(gi * blk, blk), 2 * blk)
         own = pl.ds(pl.multiple_of(gi * blk + MAXDIL * ch, MAXDIL * ch), blk)
@@ -271,11 +278,9 @@
         bsum, cs, rs = bacc[...], csum[...], rsum[...]
         for ii in range(RG):
             i = gi * RG + ii
-            side = jnp.where(i + MAXDIL >= (n // 2 // RG) * RG + RG, 1, 0)
-            v8, _ = validity(i, side)
-            v = jnp.concatenate([v8] * (ch // RG), axis=0)
+            v = jnp.concatenate([vbuf[i + MAXDIL]] * (ch // RG), axis=0)
             sl = slice(ii * ch, (ii + 1) * ch)
-            po = (hz[sl] + bias[...]) * v
+            po = (hz[sl] + bias_all) * v
             out[i] = pltpu.roll(po, lax.rem(wide - i, wide), 1)[:, :n].astype(jnp.bfloat16)
             bsum = bsum + gf[sl]
             cs = cs + dx[sl]
@@ -491,9 +496,8 @@
     )(pack, cot)
 
     blk = RG * ch
-    kf = jnp.tile(kernel.reshape(9, ch, ch), (1, 1, 4))
-    kb = jnp.tile(jnp.swapaxes(kernel.reshape(9, ch, ch), 1, 2), (1, 1, 4))
-    bias2 = jnp.broadcast_to(bias[:, None], (ch, wide))
+    kf = kernel.reshape(9, ch, ch)
+    bias2 = bias[:, None]
     nk = (9 * ch * ch) // (RG * 128) + 1
     Z = ch // RG
     out, rsum, csum, kg = pl.pallas_call(
@@ -504,7 +508,7 @@
             jax.ShapeDtypeStruct((2, Z, RG, n), f32),
             jax.ShapeDtypeStruct((nk, RG, 128), f32),
         ),
-        in_specs=[smem, smem] + [vmem] * 8,
+        in_specs=[smem, smem] + [vmem] * 7,
         out_specs=(vmem,) * 4,
         scratch_shapes=[
             pltpu.VMEM((3, ext * ch, wide), bf),
@@ -518,10 +522,11 @@
             pltpu.VMEM((ch, wide), f32),
             pltpu.VMEM((ch, n), f32),
             pltpu.VMEM((ch, wide), f32),
+            pltpu.VMEM((ext, RG, wide), f32),
         ],
         compiler_params=pltpu.CompilerParams(vmem_limit_bytes=56 * 2**20),
         name="pair_kernel",
-    )(dilation, band, near, cols, vcol, cot, halo, kf, kb, bias2)
+    )(dilation, band, near, cols, vcol, cot, halo, kf, bias2)
 
     tile = lambda *lead: pltpu.VMEM(lead + (RG, n), f32)
     embed_scale = float(T * n) ** -0.5

time: 82.3 us -> 79.8 us (0.970)
  local copies, waits for them, and re-layouts: 14.9 us -> 12.5 us
    another operation x4 -> x0, local copies, waits for them, and re-layouts: 2.69 us -> none  [the longest x2 1.79 us: local(): kf = jnp.tile(kernel.reshape(9, ch, ch), (1, 1, 4))]
    unnamed x8 -> x6, local copies, waits for them, and re-layouts: 7.68 us -> 8.9 us
    transpose x1 -> x0, local copies, waits for them, and re-layouts: 0.98 us -> none  [local(): kb = jnp.tile(jnp.swapaxes(kernel.reshape(9, ch, ch), 1, 2), (1, 1, 4))]
where the time goes in v2:
time: 79.8 us; the launch traced here: 79.2 us
  Pallas kernels  62.8 us (79%)
  local copies, waits for them, and re-layouts  12.5 us (16%)
  other arithmetic  1.98 us (2%)
  between operations  1.96 us (2%)
    pallas_call x1, Pallas kernels, local(): pl.pallas_call(pair_kernel, out_shape=(jax.ShapeDtypeStruct((n, ch, n), b...  36.6 us
    pallas_call x1, Pallas kernels, local(): pl.pallas_call(functools.partial(sum_kernel, R, T, embed_scale, weight_sc...  14.2 us
    pallas_call x1, Pallas kernels, local(): pl.pallas_call(functools.partial(gather_kernel, R, T), out_shape=(jax.Sha...  11.9 us
    unnamed x6, local copies, waits for them, and re-layouts  8.9 us

profile of v2, /device:TPU:0, one launch (start us, length us, event | category | flops | bytes accessed | tf_op | source)
XLA Modules:
  0.0 79.2 jit_solution(4560908808646368405)
XLA Ops:
  1.9 0.7 convert_element_type.3
  2.6 1.3 %pad_maximum_fusion.pack = bf16[80,128]{1,0:T(8,128)(2,1)} fusion(bf16[16,128]{1,0:T(8,128)(2,1)S(1)} %broadcast_in_dim.4, bf16[32,128]{1,0:T(8,128)(2,1)} %param.8, bf16[32,128]{1,0:T(8,128)(2,1)} %param.9), kind=kLoop, calls=%fused_computation.1 | loop fusion | flops 61440 | bytes 40960 | tf_op jit(solution)/shard_map/concatenate | solution.py:470
  3.9 1.3 %copy.23.bias = f32[32,1]{1,0:T(8,128)} copy(f32[32,1]{0,1:T(1,128)} %bitcast.19) | data formatting | bytes 256 | tf_op jit(solution)/shard_map/broadcast_in_dim | solution.py:500
  5.3 2.9 %copy.32 = bf16[32,128,128]{2,0,1:T(8,128)(2,1)} copy(bf16[32,128,128]{2,1,0:T(8,128)(2,1)} %param.12) | data formatting | bytes 2097152 | tf_op args[4]
  8.1 11.9 %gather_kernel.1 = (f32[2,32,256]{2,1,0:T(8,128)}, f32[2,8,256]{2,1,0:T(8,128)}, f32[2,40,128]{2,1,0:T(8,128)}, bf16[136,32,128]{2,1,0:T(8,128)(2,1)}, bf16[136,32,128]{2,1,0:T(8,128)(2,1)}) custom-call(bf16[80,128]{1,0:T(8,128)(2,1)} %pad_maximum_fusion.pack, bf16[128,32,128]{2,1,0:T(8,128)(2,1)} %bitcast.12), custom_call_target="tpu_custom_call" | custom-call | tf_op jit(solution)/shard_map/gather_kernel/pallas_call | solution.py:478
  20.1 36.6 %pair_kernel.1 = (bf16[128,32,128]{2,1,0:T(8,128)(2,1)}, f32[4,8,128]{2,1,0:T(8,128)}, f32[2,4,8,128]{3,2,1,0:T(8,128)}, f32[10,8,128]{2,1,0:T(8,128)}) custom-call(s32[1]{0:T(128)S(6)} %copy.35.dilation, s32[1]{0:T(128)S(6)} %copy.36.band, f32[2,40,128]{2,1,0:T(8,128)} %get-tuple-element.17.near, f32[2,32,256]{2,1,0:T(8,128)} %get-tuple-element.18.cols, ...), custom_call_target="tpu_custom_call" | custom-call | tf_op jit(solution)/shard_map/pair_kernel/pallas_call | solution.py:503
  56.7 2.6 %copy.26 = bf16[32,128,128]{2,1,0:T(8,128)(2,1)} copy(bf16[32,128,128]{2,0,1:T(8,128)(2,1)} %bitcast.13) | data formatting | bytes 2097152
  59.3 14.2 %sum_kernel.1 = (f32[10,8,128]{2,1,0:T(8,128)}, f32[32,128]{1,0:T(8,128)}, f32[32,128]{1,0:T(8,128)}) custom-call(f32[10,8,128]{2,1,0:T(8,128)} %get-tuple-element.23.kg, f32[4,8,128]{2,1,0:T(8,128)} %get-tuple-element.24.row, f32[2,4,8,128]{3,2,1,0:T(8,128)} %get-tuple-element.25.col), custom_call_target="tpu_custom_call" | custom-call | tf_op jit(solution)/shard_map/sum_kernel/pallas_call | solution.py:534
  73.5 0.7 slice.10
  74.2 0.8 slice.9
  75.0 0.1 reshape_squeeze.3
  75.0 0.1 copy.30
  75.1 0.6 reshape.26
  75.7 0.1 reshape.24
  75.9 0.7 copy.28
  76.5 1.3 %copy.37 = f32[32,128]{1,0:T(8,128)} copy(f32[32,128]{1,0:T(8,128)} %get-tuple-element.50) | data formatting | bytes 32768
  77.9 1.3 %copy.38 = f32[32,128]{1,0:T(8,128)} copy(f32[32,128]{1,0:T(8,128)} %get-tuple-element.51) | data formatting | bytes 32768
  (1 shorter events, 0.0 us)
